TPU v7x, 32 devices: a whole 2x2x4 slice. The times are simulated.
32 devices in a mesh: seq: 4 (over y, x), tp: 8 (over z, core).
Axes of the slice: x: 2, y: 2, z: 4, core: 2. Of those that a mesh axis runs over, the one named last changes fastest.
Arguments:
- activations: bfloat16 [1024, 8192], P('seq', 'tp'), may hold values from -36 to 36
- norm_gain: bfloat16 [8192], P('tp'), may hold values from 0.099609375 to 1.8984375
- in_proj: bfloat16 [8192, 3, 4096], P(None, None, 'tp'), may hold values from -0.0625 to 0.0625
- short_taps: float32 [3, 3, 4096], P(None, None, 'tp'), may hold values from -3.5 to 3.5
- medium_taps: float32 [256, 128], P('tp'), may hold values from -0.5 to 0.5
- cotangent: bfloat16 [1024, 4096], P('seq', 'tp'), may hold values from -1.1953125 to 1.1953125
Outputs:
- mixer_out: bfloat16 [1024, 4096], P('seq', 'tp')
- grad_input: bfloat16 [1024, 8192], P('seq', 'tp')
- grad_proj: bfloat16 [8192, 3, 4096], P('seq', None, 'tp')
All inputs are finite; a program needn't handle non-finite values.
Results may differ from a plain program's by a relative error of at most 0.02.
Values may be sent and summed in bfloat16 or wider, within the bound.
No kernel may reach another device: no remote copies, remote signals or barrier semaphores. Data moves between devices by JAX's collectives and lax.ppermute only.
A program may use at most 192 MiB of HBM per device.

v0:
```python
import jax
import jax.numpy as jnp
from jax import lax
from jax.sharding import PartitionSpec as P

GROUP = 16
LS = 3
LM = 128
norm_eps = 1e-06


def shifted(block, axis, distance):
    devices = range(lax.axis_size(axis))
    route = [(i - distance, i) for i in devices if i - distance in devices]
    return lax.ppermute(block, axis, route)


def forward_short(source, taps, offset, length):
    total = jnp.zeros((length,) + source.shape[1:], jnp.float32)
    for index in range(LS):
        total = total + taps[index] * source[offset - index : offset - index + length].astype(
            jnp.float32
        )
    return total


def backward_short(source, taps, length):
    total = jnp.zeros((length,) + source.shape[1:], jnp.float32)
    for index in range(LS):
        total = total + taps[index] * source[index : index + length].astype(jnp.float32)
    return total


def band_matrix(tap_rows, out_len, in_len, lead, sign):
    offsets = lead + sign * (
        lax.broadcasted_iota(jnp.int32, (out_len, in_len), 0)
        - lax.broadcasted_iota(jnp.int32, (out_len, in_len), 1)
    )
    inside = (offsets >= 0) & (offsets < LM)
    picked = jnp.take(tap_rows, jnp.clip(offsets, 0, LM - 1), axis=1)
    return jnp.where(inside[None], picked, 0.0)


def grouped_apply(band, source):
    groups_here = band.shape[0]
    shaped = source.astype(jnp.float32).reshape(source.shape[0], groups_here, GROUP)
    result = jnp.einsum("gts,sgc->tgc", band, shaped, precision=lax.Precision.HIGHEST)
    return result.reshape(band.shape[1], groups_here * GROUP)


def per_device(activations, norm_gain, in_proj, short_taps, medium_taps, cotangent):
    act_full, gain_full = (
        lax.all_gather(activations, "tp", axis=1, tiled=True),
        lax.all_gather(norm_gain, "tp", axis=0, tiled=True),
    )
    tok_rows = act_full.shape[0]
    width = act_full.shape[1]
    local_ch = in_proj.shape[2]
    edge_rows = LM + LS - 2
    head_rows = LS - 1
    act_float = act_full.astype(jnp.float32)
    inv_rms = lax.rsqrt(jnp.mean(act_float * act_float, axis=1, keepdims=True) + norm_eps)
    gain_float = gain_full.astype(jnp.float32)
    normed = (act_float * inv_rms * gain_float).astype(jnp.bfloat16)
    weight = in_proj.reshape(width, 3 * local_ch)
    projected = (
        jnp.dot(normed, weight, preferred_element_type=jnp.float32)
        .astype(jnp.bfloat16)
        .reshape(tok_rows, 3, local_ch)
    )
    kv_tail = projected[tok_rows - edge_rows :, 1:, :].reshape(edge_rows, 2 * local_ch)
    q_tail = projected[tok_rows - head_rows :, 0, :].reshape(head_rows // 2, 2 * local_ch)
    received = shifted(jnp.concatenate([kv_tail, q_tail], 0), "seq", 1)
    kv_ext = jnp.concatenate(
        [received[:edge_rows].reshape(edge_rows, 2, local_ch), projected[:, 1:, :]], 0
    )
    q_ext = jnp.concatenate(
        [received[edge_rows:].reshape(head_rows, local_ch), projected[:, 0, :]], 0
    )
    span = tok_rows + LM - 1
    kv_feat = forward_short(kv_ext, short_taps[:, 1:, :], head_rows, span).astype(jnp.bfloat16)
    q_feat = forward_short(q_ext, short_taps[:, 0, :], head_rows, tok_rows).astype(jnp.bfloat16)
    gated = (kv_feat[:, 0].astype(jnp.float32) * kv_feat[:, 1].astype(jnp.float32)).astype(
        jnp.bfloat16
    )
    band_forward = band_matrix(medium_taps, tok_rows, span, LM - 1, 1)
    filtered = grouped_apply(band_forward, gated)
    mixer_out = (q_feat.astype(jnp.float32) * filtered).astype(jnp.bfloat16)
    grad_out = cotangent.astype(jnp.float32)
    grad_filtered = (grad_out * q_feat.astype(jnp.float32)).astype(jnp.bfloat16)
    grad_q = (grad_out * filtered).astype(jnp.bfloat16)
    kv_own = kv_feat[LM - 1 :]
    front = jnp.concatenate([grad_q[:head_rows, None, :], kv_own[:head_rows]], 1)
    outgoing = jnp.concatenate(
        [grad_filtered[:edge_rows], front.reshape(3 * head_rows, local_ch)], 0
    )
    returned = shifted(outgoing, "seq", -1)
    filt_ext = jnp.concatenate([grad_filtered, returned[:edge_rows]], 0)
    front_next = returned[edge_rows:].reshape(head_rows, 3, local_ch)
    reach = tok_rows + head_rows
    band_backward = band_matrix(medium_taps, reach, tok_rows + edge_rows, 0, -1)
    grad_gated = grouped_apply(band_backward, filt_ext)
    kv_reach = jnp.concatenate([kv_own, front_next[:, 1:, :]], 0)
    q_reach = jnp.concatenate([grad_q, front_next[:, 0, :]], 0)
    grad_k = (grad_gated * kv_reach[:, 1].astype(jnp.float32)).astype(jnp.bfloat16)
    grad_v = (grad_gated * kv_reach[:, 0].astype(jnp.float32)).astype(jnp.bfloat16)
    grad_feat = jnp.stack([q_reach, grad_k, grad_v], 1)
    grad_pre = (
        backward_short(grad_feat, short_taps, tok_rows)
        .astype(jnp.bfloat16)
        .reshape(tok_rows, 3 * local_ch)
    )
    partial_grad = lax.dot_general(
        grad_pre, weight, (((1,), (1,)), ((), ())), preferred_element_type=jnp.float32
    )
    tp_count = lax.axis_size("tp")
    own_width = width // tp_count
    own_scaled = activations.astype(jnp.float32) * inv_rms
    own_gain = norm_gain.astype(jnp.float32)
    whole_grad = lax.psum(partial_grad.astype(jnp.bfloat16), "tp").astype(jnp.float32)
    stat = jnp.mean(gain_float * whole_grad * act_float, axis=1, keepdims=True) * inv_rms
    grad_slice = lax.dynamic_slice_in_dim(
        whole_grad, lax.axis_index("tp") * own_width, own_width, 1
    )
    grad_scaled = own_gain * grad_slice
    grad_input = (inv_rms * (grad_scaled - own_scaled * stat)).astype(jnp.bfloat16)
    row_share = width // lax.axis_size("seq")
    norm_cols = lax.all_to_all(normed, "seq", split_axis=1, concat_axis=0, tiled=True)
    empty = jnp.zeros((row_share, 3 * local_ch), jnp.float32)
    total = empty
    piece = lax.all_gather(grad_pre, "seq", axis=0, tiled=True)
    blocks = piece.shape[0] // tok_rows
    for block in range(blocks):
        rows = lax.dynamic_slice_in_dim(norm_cols, block * tok_rows, tok_rows, 0)
        product = lax.dot_general(
            rows,
            piece[block * tok_rows : (block + 1) * tok_rows],
            (((0,), (0,)), ((), ())),
            preferred_element_type=jnp.float32,
        ).astype(jnp.bfloat16)
        product = lax.optimization_barrier(product)
        total = total + product.astype(jnp.float32)
    grad_proj = total.reshape(row_share, 3, local_ch).astype(jnp.bfloat16)
    return (mixer_out, grad_input, grad_proj)


def solution(mesh):
    return jax.shard_map(
        per_device,
        mesh=mesh,
        in_specs=(
            P("seq", "tp"),
            P("tp"),
            P(None, None, "tp"),
            P(None, None, "tp"),
            P("tp", None),
            P("seq", "tp"),
        ),
        out_specs=(P("seq", "tp"), P("seq", "tp"), P("seq", None, "tp")),
        check_vma=False,
    )
```

profile of v0, /device:TPU:0, one launch (start us, length us, event | category | flops | bytes accessed | tf_op | source)
XLA Modules:
  0.0 788.1 jit_solution(5932457810425270629)
XLA Ops:
  7.2 0.7 all-gather.3.cloned.1.call-update
  7.9 14.6 %all_gather.10 = bf16[8192]{0:T(1024)(128)(2,1)S(1)} all-gather(bf16[1024]{0:T(1024)(128)(2,1)} %param.7), channel_id=1, replica_groups=mesh['seq'=4,'tp'=8] {'tp'}, dimensions={0}, use_global_device_ids=true | all-gather | bytes 18432 | tf_op jit(solution)/shard_map/all_gather | solution.py:54
  22.6 33.6 %copy.88 = bf16[8192,3,512]{0,2,1:T(8,128)(2,1)} copy(bf16[8192,3,512]{2,0,1:T(8,128)(2,1)} %param.8) | data formatting | bytes 50331648 | tf_op args[2]
  56.2 0.5 reshape.180
  56.9 0.5 reshape.188
  57.5 1.7 all-gather.3.cloned.1.call-done
  59.2 3.3 fusion.13
  62.7 3.2 fusion.15
  65.9 12.8 %convolution_convert_fusion.4 = bf16[256,1536]{1,0:T(8,128)(2,1)S(1)} fusion(bf16[256,8192]{1,0:T(8,128)(2,1)} %fusion.15, bf16[8192,1536]{0,1:T(8,128)(2,1)} %bitcast.91), kind=kOutput, calls=%fused_computation.33 | convolution fusion | flops 6442844160 | bytes 30146560 | tf_op jit(solution)/shard_map/dot_general | solution.py:67
  78.7 0.3 copy.89
  79.0 0.2 slice.177
  79.7 3.8 collective-permute-start
  83.8 179.7 %gather_fusion = f32[98048,32]{1,0:T(8,128)} fusion(f32[32,128]{0,1:T(8,128)S(1)} %copy.94, s32[98304]{0:T(1024)S(1)} %pad_clamp_fusion.1), kind=kCustom, calls=%fused_computation | custom fusion | bytes 25492480 | tf_op jit(solution)/shard_map/jit(_take)/gather | solution.py:40
  263.5 31.0 %copy.95 = f32[98048,32]{0,1:T(8,128)} copy(f32[98048,32]{1,0:T(8,128)} %gather_fusion) | data formatting | bytes 25100288 | tf_op jit(solution)/shard_map/jit(_take)/gather | solution.py:40
  294.5 18.2 %reshape.183 = f32[256,383,32]{1,0,2:T(8,128)} reshape(f32[98048,32]{0,1:T(8,128)} %copy.95) | data formatting | bytes 25100288 | tf_op jit(solution)/shard_map/jit(_take)/gather | solution.py:40
  312.9 0.2 copy.110
  313.1 1.7 add_convert_fusion.2
  315.3 10.1 %fusion.4 = f32[32,16,256]{2,1,0:T(8,128)S(1)} fusion(bf16[383,32,16]{0,2,1:T(8,128)(2,1)S(1)} %bitcast.104, f32[256,383,32]{1,0,2:T(8,128)} %reshape.183, pred[256,383]{1,0:T(8,128)(4,1)S(1)} %get-tuple-element.34, pred[256,383]{1,0:T(8,128)(4,1)S(1)} %get-tuple-element.33), kind=kOutput, calls=%fused_computation.6 | convolution fusion | flops 608681984 | bytes 13662720 | tf_op jit(solution)/shard_map/gts,sgc->tgc/dot_general | solution.py:47
  325.4 0.5 fusion.37
  326.2 0.2 copy.97
  326.7 1.5 collective-permute-start.1
  328.2 182.5 %gather_fusion.1 = f32[99330,32]{1,0:T(8,128)} fusion(f32[32,128]{0,1:T(8,128)S(1)} %copy.94, s32[100352]{0:T(1024)S(1)} %pad_clamp_fusion), kind=kCustom, calls=%fused_computation.1 | custom fusion | bytes 25825800 | tf_op jit(solution)/shard_map/jit(_take)/gather | solution.py:40
  510.8 31.5 %copy.102 = f32[99330,32]{0,1:T(8,128)} copy(f32[99330,32]{1,0:T(8,128)} %gather_fusion.1) | data formatting | bytes 25428480 | tf_op jit(solution)/shard_map/jit(_take)/gather | solution.py:40
  542.3 30.9 %reshape.191 = f32[258,385,32]{1,0,2:T(8,128)} reshape(f32[99330,32]{0,1:T(8,128)} %copy.102) | data formatting | bytes 25428480 | tf_op jit(solution)/shard_map/jit(_take)/gather | solution.py:40
  573.1 0.4 fusion.33
  573.5 0.2 slice.196
  574.3 0.2 copy.112
  574.5 14.0 %fusion = f32[32,16,258]{2,1,0:T(8,128)S(1)} fusion(bf16[385,32,16]{0,2,1:T(8,128)(2,1)S(1)} %bitcast.101, f32[258,385,32]{1,0,2:T(8,128)} %reshape.191, pred[258,385]{1,0:T(8,128)(4,1)S(1)} %get-tuple-element.36, pred[258,385]{1,0:T(8,128)(4,1)S(1)} %get-tuple-element.35), kind=kOutput, calls=%fused_computation.2 | convolution fusion | flops 616640640 | bytes 13835524 | tf_op jit(solution)/shard_map/gts,sgc->tgc/dot_general | solution.py:47
  588.8 0.3 pad_maximum_fusion
  589.0 1.2 add_convert_fusion.1
  590.3 13.3 %fusion.8 = bf16[256,8192]{1,0:T(8,128)(2,1)} fusion(bf16[256,3,512]{0,2,1:T(8,128)(2,1)S(1)} %add_convert_fusion.1, bf16[8192,3,512]{2,0,1:T(8,128)(2,1)} %param.8), kind=kOutput, calls=%fused_computation.15 | convolution fusion | flops 6444548096 | bytes 30146560 | tf_op jit(solution)/shard_map/dot_general | solution.py:113
  603.6 0.7 all-gather.5.cloned.1.call-update
  604.3 4.8 copy.116
  609.1 5.2 all-to-all-start
  614.4 0.8 copy.107
  615.2 85.0 %all-reduce.2.cloned.1.call-done = bf16[256,8192]{1,0:T(8,128)(2,1)} async-done(((bf16[256,8192]{1,0:T(8,128)(2,1)}), bf16[256,8192]{1,0:T(8,128)(2,1)}) %all-reduce.2.cloned.1.call-update) | async-done | bytes 4194320 | tf_op jit(solution)/shard_map/psum | solution.py:120
  700.2 3.3 convert_element_type.175
  703.6 1.3 copy-done.2
  704.9 1.7 fusion.16
  706.6 1.1 multiply_convert_fusion
  707.7 38.1 %all-gather.5.cloned.1.call-done = bf16[1024,1536]{0,1:T(8,128)(2,1)} async-done(((bf16[256,1536]{0,1:T(8,128)(2,1)}), bf16[1024,1536]{0,1:T(8,128)(2,1)}) %all-gather.5.cloned.1.call-update) | async-done | bytes 3145744 | tf_op jit(solution)/shard_map/all_gather | solution.py:131
  745.8 3.5 convolution_convert_fusion.3
  749.3 3.1 convolution_convert_fusion.2
  752.4 3.1 convolution_convert_fusion.1
  755.5 3.1 convolution_convert_fusion
  758.6 5.3 add_convert_fusion
  763.8 8.7 %copy.106 = bf16[2048,1536]{0,1:T(8,128)(2,1)} copy(bf16[2048,1536]{1,0:T(8,128)(2,1)} %add_convert_fusion) | data formatting | bytes 12582912 | tf_op jit(solution)/shard_map/convert_element_type | solution.py:143
  772.6 8.6 %copy.108 = bf16[2048,3,512]{2,0,1:T(8,128)(2,1)} copy(bf16[2048,3,512]{0,2,1:T(8,128)(2,1)} %bitcast.92) | data formatting | bytes 12582912
  (79 shorter events, 3.5 us)
Async XLA Ops:
  7.2 52.0 %all-gather.3.cloned.1.call-start = ((), (), s32[]{:S(2)}) async-start(), calls=%async_computation.1 | async-start | bytes 4718592 | tf_op jit(solution)/shard_map/all_gather | solution.py:53
  7.9 692.3 %all-reduce.2.cloned.1.call-start = ((), (), s32[]{:S(2)}) async-start(), calls=%async_computation.2 | async-start | bytes 8388608 | tf_op jit(solution)/shard_map/psum | solution.py:120
  22.6 39.9 %copy-start.6 = (f32[8192]{0:T(1024)}, f32[8192]{0:T(1024)S(1)}, u32[]{:S(2)}) copy-start(f32[8192]{0:T(1024)S(1)} %convert_element_type.145) | copy-start | bytes 98308
  22.6 34.8 %copy-start.9 = (f32[3,3,512]{2,1,0:T(4,128)S(1)}, f32[3,3,512]{2,1,0:T(4,128)}, u32[]{:S(2)}) copy-start(f32[3,3,512]{2,1,0:T(4,128)} %param.9) | copy-start | bytes 55300
  59.2 3.4 copy-start
  62.5 16.2 %copy-start.13 = (f32[256]{0:T(256)}, f32[256]{0:T(256)S(1)}, u32[]{:S(2)}) copy-start(f32[256]{0:T(256)S(1)} %fusion.13) | copy-start | bytes 3076
  62.7 16.0 %copy-start.11 = (f32[256]{0:T(256)}, f32[256]{0:T(256)S(1)}, u32[]{:S(2)}) copy-start(f32[256]{0:T(256)S(1)} %add_rsqrt_fusion) | copy-start | bytes 3076
  65.8 17.9 %copy-start.10 = (f32[32,128]{1,0:T(8,128)S(1)}, f32[32,128]{1,0:T(8,128)}, u32[]{:S(2)}) copy-start(f32[32,128]{1,0:T(8,128)} %param.10) | copy-start | bytes 49156
  79.7 233.3 %collective-permute-start = (bf16[130,1024]{1,0:T(8,128)(2,1)S(1)}, bf16[130,1024]{1,0:T(8,128)(2,1)S(1)}, u32[]{:S(2)}, u32[]{:S(2)}) collective-permute-start(bf16[130,1024]{1,0:T(8,128)(2,1)S(1)} %pad_maximum_fusion.5), channel_id=1, source_target_pairs={{0,8},{8,16},{16,24},{1,9},{9,17},{17,25},{2,10},{10,18},{18,26},{... | collective-permute-start | bytes 798728 | tf_op jit(solution)/shard_map/ppermute | solution.py:15
  294.5 18.2 %copy-start.8 = (bf16[256,512]{1,0:T(8,128)(2,1)S(1)}, bf16[256,512]{1,0:T(8,128)(2,1)}, u32[]{:S(2)}) copy-start(bf16[256,512]{1,0:T(8,128)(2,1)} %param.11) | copy-start | bytes 786436
  326.7 247.0 %collective-permute-start.1 = (bf16[135,512]{0,1:T(8,128)(2,1)S(1)}, bf16[135,512]{0,1:T(8,128)(2,1)S(1)}, u32[]{:S(2)}, u32[]{:S(2)}) collective-permute-start(bf16[135,512]{0,1:T(8,128)(2,1)S(1)} %pad_maximum_fusion.7), channel_id=1, source_target_pairs={{8,0},{16,8},{24,16},{9,1},{17,9},{25,17},{10,2},{18,10},{26,18},{... | collective-permute-start | bytes 414728 | tf_op jit(solution)/shard_map/ppermute | solution.py:15
  590.3 13.3 %copy-start.4 = (bf16[256,3,512]{0,2,1:T(8,128)(2,1)}, bf16[256,3,512]{0,2,1:T(8,128)(2,1)S(1)}, u32[]{:S(2)}) copy-start(bf16[256,3,512]{0,2,1:T(8,128)(2,1)S(1)} %add_convert_fusion.1) | copy-start | bytes 2359300
  603.6 142.2 %all-gather.5.cloned.1.call-start = ((), (), s32[]{:S(2)}) async-start(), calls=%async_computation.3 | async-start | bytes 3932160 | tf_op jit(solution)/shard_map/all_gather | solution.py:131
  609.1 5.2 copy-start.15
  609.1 98.6 %all-to-all-start = ((bf16[256,4,2048]{2,0,1:T(8,128)(2,1)}), bf16[256,4,2048]{2,0,1:T(8,128)(2,1)}, u32[]{:S(2)}, u32[]{:S(2)}) async-start(bf16[256,4,2048]{2,0,1:T(8,128)(2,1)} %bitcast.94), calls=%async_computation | async-start | bytes 8388608 | tf_op jit(solution)/shard_map/all_to_all | solution.py:128
  615.2 88.3 %copy-start.7 = (f32[8192]{0:T(1024)S(1)}, f32[8192]{0:T(1024)}, u32[]{:S(2)}) copy-start(f32[8192]{0:T(1024)} %copy-done.6) | copy-start | bytes 98308
  700.2 3.4 copy-start.1
  700.2 4.7 copy-start.2
  704.9 1.7 copy-start.14
  704.9 1.7 copy-start.5
  704.9 1.7 copy-start.12
  745.8 3.5 copy-start.3
Sparse Core Ops, SparseCore 0:
  9.6 49.5 all-gather.2
  603.7 96.4 all-reduce.1
  702.0 43.7 all-gather.4
where the time goes:
time: 797 us; the launch traced here: 788 us
  local copies, waits for them, and re-layouts  536 us (67%)
  waiting for transfers between devices  126 us (16%)
  matrix products  62.9 us (8%)
  other arithmetic  23.1 us (3%)
  blocking collectives  14.6 us (2%)
  between operations  14.6 us (2%)
  starting transfers between devices  10.6 us (1%)
    gather x6, local copies, waits for them, and re-layouts, band_matrix(): picked = jnp.take(tap_rows, jnp.clip(offsets, 0, LM - 1), axis=1)  474 us
    psum x1, waiting for transfers between devices, per_device(): lax.psum(partial_grad.astype(jnp.bfloat16), 'tp').astype(jnp.float32)  85 us
    unnamed x40, local copies, waits for them, and re-layouts  45.3 us
    all_gather x1, waiting for transfers between devices, per_device(): piece = lax.all_gather(grad_pre, 'seq', axis=0, tiled=True)  38.1 us
    dot_general x2, matrix products, grouped_apply(): jnp.einsum('gts,sgc->tgc', band, shaped, precision=lax.Precision.HIGHEST)  24.1 us
  transfers between devices with their start and end apart: 6, of which 3 were waited for; matrix products, arithmetic and copies ran while one was open for 66% of the time, Pallas kernels for 0%

commit v1 on v0

--- a/solution.py
+++ b/solution.py
@@ -117,7 +117,9 @@
     own_width = width // tp_count
     own_scaled = activations.astype(jnp.float32) * inv_rms
     own_gain = norm_gain.astype(jnp.float32)
-    whole_grad = lax.psum(partial_grad.astype(jnp.bfloat16), "tp").astype(jnp.float32)
+    whole_grad = jnp.sum(lax.all_gather(partial_grad.astype(jnp.bfloat16), "tp"), axis=0).astype(
+        jnp.float32
+    )
     stat = jnp.mean(gain_float * whole_grad * act_float, axis=1, keepdims=True) * inv_rms
     grad_slice = lax.dynamic_slice_in_dim(
         whole_grad, lax.axis_index("tp") * own_width, own_width, 1

time: 797 us -> 1000 us (1.25)
  waiting for transfers between devices: 126 us -> 313 us
  other arithmetic: 23.1 us -> 38.2 us
    all_gather x0 -> x1, waiting for transfers between devices: none -> 248 us  [per_device(): lax.all_gather(partial_grad.astype(jnp.bfloat16), 'tp')]
    psum x1 -> x0, waiting for transfers between devices: 85 us -> none  [per_device(): lax.psum(partial_grad.astype(jnp.bfloat16), 'tp').astype(jnp.float32)]
    all_to_all x1, waiting for transfers between devices: 0.01 us -> 61.9 us  [per_device(): lax.all_to_all(normed, 'seq', split_axis=1, concat_axis=0, tiled=True)]
    all_gather x1, waiting for transfers between devices: 38.1 us -> 0.01 us  [per_device(): piece = lax.all_gather(grad_pre, 'seq', axis=0, tiled=True)]
    reduce_sum x0 -> x1, other arithmetic: none -> 14.3 us  [per_device(): jnp.sum(lax.all_gather(partial_grad.astype(jnp.bfloat16), 'tp'), axis=0)]
    unnamed x40 -> x38, local copies, waits for them, and re-layouts: 45.3 us -> 44.2 us
  transfers between devices with their start and end apart: 6 -> 6, of which waited for: 3 -> 3; matrix products, arithmetic and copies ran while one was open for 66% -> 57% of each run, Pallas kernels for 0% -> 0%
where the time goes in v1:
time: 1000 us; the launch traced here: 993 us
  local copies, waits for them, and re-layouts  538 us (54%)
  waiting for transfers between devices  313 us (31%)
  matrix products  64.1 us (6%)
  other arithmetic  38.2 us (4%)
  blocking collectives  14.6 us (1%)
  between operations  14.4 us (1%)
  starting transfers between devices  10.7 us (1%)
    gather x6, local copies, waits for them, and re-layouts, band_matrix(): picked = jnp.take(tap_rows, jnp.clip(offsets, 0, LM - 1), axis=1)  475 us
    all_gather x1, waiting for transfers between devices, per_device(): lax.all_gather(partial_grad.astype(jnp.bfloat16), 'tp')  248 us
    all_to_all x1, waiting for transfers between devices, per_device(): lax.all_to_all(normed, 'seq', split_axis=1, concat_axis=0, tiled=True)  61.9 us
    unnamed x38, local copies, waits for them, and re-layouts  44.2 us
    dot_general x2, matrix products, grouped_apply(): jnp.einsum('gts,sgc->tgc', band, shaped, precision=lax.Precision.HIGHEST)  24.1 us
  transfers between devices with their start and end apart: 6, of which 3 were waited for; matrix products, arithmetic and copies ran while one was open for 57% of the time, Pallas kernels for 0%

profile of v1, /device:TPU:0, one launch (start us, length us, event | category | flops | bytes accessed | tf_op | source)
XLA Modules:
  0.0 993.2 jit_solution(52375864635151756)
XLA Ops:
  7.2 0.7 all-gather.5.cloned.1.call-update
  7.9 14.6 %all_gather.16 = bf16[8192]{0:T(1024)(128)(2,1)S(1)} all-gather(bf16[1024]{0:T(1024)(128)(2,1)} %param.7), channel_id=1, replica_groups=mesh['seq'=4,'tp'=8] {'tp'}, dimensions={0}, use_global_device_ids=true | all-gather | bytes 18432 | tf_op jit(solution)/shard_map/all_gather | solution.py:54
  22.6 32.5 %copy.97 = bf16[8192,3,512]{0,2,1:T(8,128)(2,1)} copy(bf16[8192,3,512]{2,0,1:T(8,128)(2,1)} %param.8) | data formatting | bytes 50331648 | tf_op args[2]
  55.1 0.5 reshape.180
  55.8 0.5 reshape.188
  56.4 2.8 all-gather.5.cloned.1.call-done
  59.2 3.3 fusion.13
  62.7 3.2 fusion.15
  65.9 12.8 %convolution_convert_fusion.4 = bf16[256,1536]{1,0:T(8,128)(2,1)S(1)} fusion(bf16[256,8192]{1,0:T(8,128)(2,1)} %fusion.15, bf16[8192,1536]{0,1:T(8,128)(2,1)} %bitcast.94), kind=kOutput, calls=%fused_computation.32 | convolution fusion | flops 6442844160 | bytes 30146560 | tf_op jit(solution)/shard_map/dot_general | solution.py:67
  78.7 0.3 copy.98
  79.0 0.2 slice.177
  79.7 3.6 collective-permute-start
  83.5 180.3 %gather_fusion = f32[98048,32]{1,0:T(8,128)} fusion(f32[32,128]{0,1:T(8,128)S(1)} %copy.103, s32[98304]{0:T(1024)S(1)} %pad_clamp_fusion.1), kind=kCustom, calls=%fused_computation | custom fusion | bytes 25492480 | tf_op jit(solution)/shard_map/jit(_take)/gather | solution.py:40
  263.8 31.0 %copy.104 = f32[98048,32]{0,1:T(8,128)} copy(f32[98048,32]{1,0:T(8,128)} %gather_fusion) | data formatting | bytes 25100288 | tf_op jit(solution)/shard_map/jit(_take)/gather | solution.py:40
  294.8 18.2 %reshape.183 = f32[256,383,32]{1,0,2:T(8,128)} reshape(f32[98048,32]{0,1:T(8,128)} %copy.104) | data formatting | bytes 25100288 | tf_op jit(solution)/shard_map/jit(_take)/gather | solution.py:40
  313.5 1.7 add_convert_fusion.2
  315.7 10.1 %fusion.4 = f32[32,16,256]{2,1,0:T(8,128)S(1)} fusion(bf16[383,32,16]{0,2,1:T(8,128)(2,1)S(1)} %bitcast.106, f32[256,383,32]{1,0,2:T(8,128)} %reshape.183, pred[256,383]{1,0:T(8,128)(4,1)S(1)} %get-tuple-element.34, pred[256,383]{1,0:T(8,128)(4,1)S(1)} %get-tuple-element.33), kind=kOutput, calls=%fused_computation.6 | convolution fusion | flops 608681984 | bytes 13662720 | tf_op jit(solution)/shard_map/gts,sgc->tgc/dot_general | solution.py:47
  325.8 0.5 fusion.37
  326.5 0.2 copy.106
  327.1 1.5 collective-permute-start.1
  328.6 183.2 %gather_fusion.1 = f32[99330,32]{1,0:T(8,128)} fusion(f32[32,128]{0,1:T(8,128)S(1)} %copy.103, s32[100352]{0:T(1024)S(1)} %pad_clamp_fusion), kind=kCustom, calls=%fused_computation.1 | custom fusion | bytes 25825800 | tf_op jit(solution)/shard_map/jit(_take)/gather | solution.py:40
  511.8 31.5 %copy.111 = f32[99330,32]{0,1:T(8,128)} copy(f32[99330,32]{1,0:T(8,128)} %gather_fusion.1) | data formatting | bytes 25428480 | tf_op jit(solution)/shard_map/jit(_take)/gather | solution.py:40
  543.3 30.9 %reshape.191 = f32[258,385,32]{1,0,2:T(8,128)} reshape(f32[99330,32]{0,1:T(8,128)} %copy.111) | data formatting | bytes 25428480 | tf_op jit(solution)/shard_map/jit(_take)/gather | solution.py:40
  574.2 0.4 fusion.33
  574.5 0.2 slice.196
  575.4 0.2 copy.125
  575.6 14.0 %fusion = f32[32,16,258]{2,1,0:T(8,128)S(1)} fusion(bf16[385,32,16]{0,2,1:T(8,128)(2,1)S(1)} %bitcast.103, f32[258,385,32]{1,0,2:T(8,128)} %reshape.191, pred[258,385]{1,0:T(8,128)(4,1)S(1)} %get-tuple-element.36, pred[258,385]{1,0:T(8,128)(4,1)S(1)} %get-tuple-element.35), kind=kOutput, calls=%fused_computation.2 | convolution fusion | flops 616640640 | bytes 13835524 | tf_op jit(solution)/shard_map/gts,sgc->tgc/dot_general | solution.py:47
  589.8 0.3 pad_maximum_fusion
  590.0 2.0 add_convert_fusion.1
  592.1 0.4 all-gather.9.cloned.1.call-start
  592.5 13.9 %fusion.8 = bf16[256,8192]{1,0:T(8,128)(2,1)} fusion(bf16[256,3,512]{0,2,1:T(8,128)(2,1)} %add_convert_fusion.1, bf16[8192,3,512]{2,0,1:T(8,128)(2,1)} %param.8), kind=kOutput, calls=%fused_computation.15 | convolution fusion | flops 6444548096 | bytes 30146560 | tf_op jit(solution)/shard_map/dot_general | solution.py:113
  606.4 6.4 copy.114
  612.8 5.1 all-to-all-start
  618.0 0.8 copy.120
  618.8 61.9 %all-to-all-done = bf16[256,4,2048]{0,2,1:T(8,128)(2,1)} async-done(((bf16[256,4,2048]{0,2,1:T(8,128)(2,1)}), bf16[256,4,2048]{0,2,1:T(8,128)(2,1)}, u32[]{:S(2)}, u32[]{:S(2)}) %all-to-all-start) | async-done | bytes 4194336 | tf_op jit(solution)/shard_map/all_to_all | solution.py:130
  680.7 3.4 convolution_convert_fusion.3
  684.2 3.2 convolution_convert_fusion.2
  687.4 3.3 convolution_convert_fusion.1
  690.7 3.4 convolution_convert_fusion
  694.1 5.3 add_convert_fusion
  699.4 8.8 copy.119
  708.2 8.6 copy.121
  716.8 247.9 %all-gather.9.cloned.1.call-done = bf16[2048,8192]{1,0:T(8,128)(2,1)} async-done(((bf16[256,8192]{1,0:T(8,128)(2,1)}), bf16[2048,8192]{1,0:T(8,128)(2,1)}) %all-gather.9.cloned.1.call-update) | async-done | bytes 33554448 | tf_op jit(solution)/shard_map/all_gather | solution.py:120
  964.7 14.3 %reduce_sum.31 = bf16[256,8192]{1,0:T(8,128)(2,1)} reduce(bf16[8,256,8192]{2,1,0:T(8,128)(2,1)} %bitcast.93, bf16[]{:T(256)} %constant.30.clone.1), dimensions={0}, to_apply=%region_1.2 | reduce | flops 14680064 | bytes 37748736 | tf_op jit(solution)/shard_map/reduce_sum | solution.py:120
  979.0 3.3 convert_element_type.177
  982.5 1.3 copy-done.2
  983.8 1.6 fusion.16
  985.4 1.1 multiply_convert_fusion
  (78 shorter events, 3.6 us)
Async XLA Ops:
  7.2 52.0 %all-gather.5.cloned.1.call-start = ((), (), s32[]{:S(2)}) async-start(), calls=%async_computation.1 | async-start | bytes 4718592 | tf_op jit(solution)/shard_map/all_gather | solution.py:53
  7.9 672.8 %all-gather.7.cloned.1.call-start = ((), (), s32[]{:S(2)}) async-start(), calls=%async_computation.2 | async-start | bytes 3932160 | tf_op jit(solution)/shard_map/all_gather | solution.py:133
  22.6 39.9 %copy-start.5 = (f32[8192]{0:T(1024)}, f32[8192]{0:T(1024)S(1)}, u32[]{:S(2)}) copy-start(f32[8192]{0:T(1024)S(1)} %convert_element_type.147) | copy-start | bytes 98308
  22.6 33.7 %copy-start.8 = (f32[3,3,512]{2,1,0:T(4,128)S(1)}, f32[3,3,512]{2,1,0:T(4,128)}, u32[]{:S(2)}) copy-start(f32[3,3,512]{2,1,0:T(4,128)} %param.9) | copy-start | bytes 55300
  59.2 3.4 copy-start.1
  62.5 16.2 %copy-start.12 = (f32[256]{0:T(256)}, f32[256]{0:T(256)S(1)}, u32[]{:S(2)}) copy-start(f32[256]{0:T(256)S(1)} %fusion.13) | copy-start | bytes 3076
  62.7 16.0 %copy-start.10 = (f32[256]{0:T(256)}, f32[256]{0:T(256)S(1)}, u32[]{:S(2)}) copy-start(f32[256]{0:T(256)S(1)} %add_rsqrt_fusion) | copy-start | bytes 3076
  65.8 17.6 %copy-start.9 = (f32[32,128]{1,0:T(8,128)S(1)}, f32[32,128]{1,0:T(8,128)}, u32[]{:S(2)}) copy-start(f32[32,128]{1,0:T(8,128)} %param.10) | copy-start | bytes 49156
  79.7 233.6 %collective-permute-start = (bf16[130,1024]{1,0:T(8,128)(2,1)S(1)}, bf16[130,1024]{1,0:T(8,128)(2,1)S(1)}, u32[]{:S(2)}, u32[]{:S(2)}) collective-permute-start(bf16[130,1024]{1,0:T(8,128)(2,1)S(1)} %pad_maximum_fusion.5), channel_id=1, source_target_pairs={{0,8},{8,16},{16,24},{1,9},{9,17},{17,25},{2,10},{10,18},{18,26},{... | collective-permute-start | bytes 798728 | tf_op jit(solution)/shard_map/ppermute | solution.py:15
  294.8 18.2 %copy-start.7 = (bf16[256,512]{1,0:T(8,128)(2,1)S(1)}, bf16[256,512]{1,0:T(8,128)(2,1)}, u32[]{:S(2)}) copy-start(bf16[256,512]{1,0:T(8,128)(2,1)} %param.11) | copy-start | bytes 786436
  327.1 247.7 %collective-permute-start.1 = (bf16[135,512]{0,1:T(8,128)(2,1)S(1)}, bf16[135,512]{0,1:T(8,128)(2,1)S(1)}, u32[]{:S(2)}, u32[]{:S(2)}) collective-permute-start(bf16[135,512]{0,1:T(8,128)(2,1)S(1)} %pad_maximum_fusion.7), channel_id=1, source_target_pairs={{8,0},{16,8},{24,16},{9,1},{17,9},{25,17},{10,2},{18,10},{26,18},{... | collective-permute-start | bytes 414728 | tf_op jit(solution)/shard_map/ppermute | solution.py:15
  592.1 372.6 %all-gather.9.cloned.1.call-start = ((), (), s32[]{:S(2)}) async-start(), calls=%async_computation.3 | async-start | bytes 37748736 | tf_op jit(solution)/shard_map/all_gather | solution.py:120
  612.8 5.1 copy-start.14
  612.8 67.9 %all-to-all-start = ((bf16[256,4,2048]{0,2,1:T(8,128)(2,1)}), bf16[256,4,2048]{0,2,1:T(8,128)(2,1)}, u32[]{:S(2)}, u32[]{:S(2)}) async-start(bf16[256,4,2048]{0,2,1:T(8,128)(2,1)} %bitcast.96), calls=%async_computation | async-start | bytes 8388608 | tf_op jit(solution)/shard_map/all_to_all | solution.py:130
  680.7 3.4 copy-start.3
  979.0 3.4 copy-start
  979.0 4.7 copy-start.2
  979.0 4.7 copy-start.6
  983.8 1.6 copy-start.13
  983.8 1.6 copy-start.4
  983.8 1.6 copy-start.11
Sparse Core Ops, SparseCore 0:
  9.6 49.5 all-gather.4
  592.2 79.5 all-gather.6
  673.4 291.1 all-gather.8
